TPU v7x, 256 devices: a whole 4x4x8 slice. The times are simulated.
256 devices in a mesh: grid: 64 (over z, y, core), lev: 4 (over x).
Axes of the slice: x: 4, y: 4, z: 8, core: 2. Of those that a mesh axis runs over, the one named last changes fastest.
Arguments:
- prior_fields: float32 [128, 8, 32768], P('grid', 'lev'), may hold values from -6 to 6
- channel_weights: float32 [8, 4], P('lev'), may hold values from 0.1 to 1
- obs_owner: int32 [4], replicated, may hold values from 0 to 63
- obs_offset: int32 [4, 4, 64], replicated, may hold values from 0 to 511
- obs_value: float32 [4, 4, 64], P(None, 'lev'), may hold values from -30 to 30
- obs_error: float32 [4, 4, 64], P(None, 'lev'), may hold values from 0.5 to 2
- ancestors: int32 [4, 4, 64, 128], P(None, 'lev', 'grid'), may hold values from 0 to 127
Outputs:
- posterior_fields: float32 [128, 8, 32768], P('grid', 'lev')
All inputs are finite; a program needn't handle non-finite values.
Results may differ from a plain program's by a relative error of at most 0.0003.
Values sent between devices are 32-bit elements; how exact they have to be, the bound alone decides.
A program may use at most 128 MiB of HBM per device.

v0:
```python
import jax
import jax.numpy as jnp
from jax import lax
from jax.sharding import PartitionSpec as P

NB = 4
HIGH = lax.Precision.HIGHEST


def spread(value, axis, source):
    kept = jnp.where(lax.axis_index(axis) == source, value, 0).astype(value.dtype)
    return lax.psum(kept, axis)


def blend_matrices(prior_obs, observed, obs_dev, centres, positions, scale, parents):
    count = observed.shape[0]
    members = prior_obs.shape[1]
    innovation = ((observed[:, None] - prior_obs) / obs_dev[:, None]) ** 2
    distance = (centres[:, None] - positions[None, :]) / scale
    taper = jnp.exp(-0.5 * distance * distance)
    log_weight = -0.5 / count * jnp.dot(taper, innovation, precision=HIGH)
    top_value = jnp.max(log_weight, axis=1, keepdims=True)
    expo_weight = jnp.exp(log_weight - top_value)
    weight = expo_weight / jnp.sum(expo_weight, axis=1, keepdims=True)
    alpha = 0.8 * (1.0 - jnp.exp(-jnp.sum(taper, axis=1) / count))
    onehot = (parents[:, :, None] == jnp.arange(members, dtype=jnp.int32)[None, None, :]).astype(
        jnp.float32
    )
    identity = jnp.eye(members, dtype=jnp.float32)
    remain = 1.0 - alpha
    return (
        alpha[:, None, None] * onehot
        + remain[:, None, None] * identity[None]
        + (weight - 1.0 / members)[:, None, :]
    )


def body(prior_fields, channel_weights, obs_owner, obs_offset, obs_value, obs_error, ancestors):
    grid_count = lax.axis_size("grid")
    member_slab, group_depth, cells = prior_fields.shape
    members = member_slab * grid_count
    block_cells = cells // grid_count
    local_regions = ancestors.shape[2]
    region_cells = block_cells // local_regions
    scale = local_regions * grid_count / 2.0
    groups = channel_weights.shape[1]
    count = obs_offset.shape[2]
    group = lax.axis_index("lev")
    block = lax.axis_index("grid")
    region_list = jnp.arange(local_regions, dtype=jnp.int32)
    centres = (block * local_regions + region_list).astype(jnp.float32) + 0.5
    first_cells = obs_offset[0].reshape(-1)
    fields = lax.all_to_all(prior_fields, "grid", split_axis=2, concat_axis=0, tiled=True)
    picked = fields[:, :, first_cells]
    for batch in range(NB):
        owner = obs_owner[batch]
        if batch > 0:
            picked = fields[:, :, obs_offset[batch].reshape(-1)]
        partial_value = jnp.einsum(
            "mlgk,lg->gkm",
            picked.reshape(members, group_depth, groups, count),
            channel_weights,
            precision=HIGH,
        )
        shared = spread(partial_value, "grid", owner)
        priors = lax.psum(shared, "lev")
        own_priors = lax.dynamic_index_in_dim(priors, group, 0, keepdims=False)
        own_offsets = lax.dynamic_index_in_dim(obs_offset[batch], group, 0, keepdims=False)
        positions = (owner * block_cells + own_offsets).astype(jnp.float32) / region_cells
        blend = blend_matrices(
            own_priors,
            obs_value[batch, 0],
            obs_error[batch, 0],
            centres,
            positions,
            scale,
            ancestors[batch, 0],
        )
        slab = fields.reshape(members, group_depth, local_regions, region_cells)
        mixed = jnp.einsum("rjm,mlrc->jlrc", blend, slab, precision=HIGH)
        fields = mixed.reshape(members, group_depth, block_cells)
    return lax.all_to_all(fields, "grid", split_axis=0, concat_axis=2, tiled=True)


def solution(mesh):
    in_specs = (
        P("grid", "lev", None),
        P("lev", None),
        P(),
        P(),
        P(None, "lev", None),
        P(None, "lev", None),
        P(None, "lev", "grid", None),
    )
    out_specs = P("grid", "lev", None)
    return jax.shard_map(body, mesh=mesh, in_specs=in_specs, out_specs=out_specs, check_vma=False)
```

profile of v0, /device:TPU:1, one launch (start us, length us, event | category | flops | bytes accessed | tf_op | source)
XLA Modules:
  0.0 1151.4 jit_solution(4428390036950253252)
XLA Ops:
  6.5 32.4 %copy.30 = f32[2,2,32768]{1,0,2:T(2,128)} copy(f32[2,2,32768]{2,1,0:T(2,128)} %param.7) | data formatting | bytes 1048576 | tf_op args[0]
  39.0 49.5 %reshape.797 = f32[64,1,2048]{2,1,0:T(1,128)} reshape(f32[32768,2,2]{2,1,0:T(2,128)} %bitcast.174) | data formatting | bytes 1048576
  88.5 13.2 %all-to-all-start = ((f32[64,1,2048]{2,1,0:T(1,128)}), f32[64,1,2048]{2,1,0:T(1,128)S(1)}, u32[]{:S(2)}, u32[]{:S(2)}) async-start(f32[64,1,2048]{2,1,0:T(1,128)} %reshape.797), calls=%async_computation | async-start | bytes 1048576 | tf_op jit(solution)/shard_map/all_to_all | solution.py:53
  101.9 0.7 fusion.106
  103.3 16.1 %all-to-all-done = f32[64,1,2048]{2,1,0:T(1,128)S(1)} async-done(((f32[64,1,2048]{2,1,0:T(1,128)}), f32[64,1,2048]{2,1,0:T(1,128)S(1)}, u32[]{:S(2)}, u32[]{:S(2)}) %all-to-all-start) | async-done | bytes 524320 | tf_op jit(solution)/shard_map/all_to_all | solution.py:53
  119.4 0.5 broadcast.610
  119.9 1.9 reduce.32
  121.8 53.4 %reshape.798 = f32[32768,2,2]{2,1,0:T(2,128)} reshape(f32[64,2048]{1,0:T(8,128)S(1)} %reduce.32) | data formatting | bytes 1048576
  175.2 35.6 %copy.31 = f32[2,2,64,512]{3,0,2,1:T(2,128)S(1)} copy(f32[2,2,64,512]{1,0,3,2:T(2,128)} %bitcast.173) | data formatting | bytes 1048576 | tf_op jit(solution)/shard_map/all_to_all | solution.py:53
  211.5 1.0 gather_fusion
  212.6 0.7 select_bitcast_fusion.3
  214.0 169.1 %all-reduce.9.cloned.1.call-done = f32[4,64,128]{2,1,0:T(8,128)} async-done(((f32[4,64,128]{2,1,0:T(8,128)}), f32[4,64,128]{2,1,0:T(8,128)}) %all-reduce.9.cloned.1.call-update) | async-done | bytes 131088 | tf_op jit(solution)/shard_map/psum | solution.py:12
  383.2 0.6 fusion.104
  385.4 41.5 %all-reduce.11.cloned.1.call-done = f32[4,64,128]{2,1,0:T(8,128)} async-done(((f32[4,64,128]{2,1,0:T(8,128)}), f32[4,64,128]{2,1,0:T(8,128)}) %all-reduce.11.cloned.1.call-update) | async-done | bytes 131088 | tf_op jit(solution)/shard_map/psum | solution.py:66
  426.9 1.6 fusion.107
  428.4 1.3 fusion.97
  429.8 1.3 divide_add_fusion.3
  431.1 0.6 fusion.7
  432.0 1.0 gather_fusion.1
  433.1 0.7 select_bitcast_fusion.2
  434.5 175.3 %all-reduce.13.cloned.1.call-done = f32[4,64,128]{2,1,0:T(8,128)} async-done(((f32[4,64,128]{2,1,0:T(8,128)}), f32[4,64,128]{2,1,0:T(8,128)}) %all-reduce.13.cloned.1.call-update) | async-done | bytes 131088 | tf_op jit(solution)/shard_map/psum | solution.py:12
  610.1 0.6 fusion.103
  612.1 41.4 %all-reduce.15.cloned.1.call-done = f32[4,64,128]{2,1,0:T(8,128)} async-done(((f32[4,64,128]{2,1,0:T(8,128)}), f32[4,64,128]{2,1,0:T(8,128)}) %all-reduce.15.cloned.1.call-update) | async-done | bytes 131088 | tf_op jit(solution)/shard_map/psum | solution.py:66
  653.5 1.6 fusion.108
  655.1 1.3 fusion.98
  656.4 1.3 divide_add_fusion.2
  657.8 1.0 convolution_bitcast_fusion.2
  658.8 0.4 copy.37
  659.2 1.0 gather_fusion.2
  660.6 0.7 select_bitcast_fusion.1
  662.0 175.4 %all-reduce.17.cloned.1.call-done = f32[4,64,128]{2,1,0:T(8,128)} async-done(((f32[4,64,128]{2,1,0:T(8,128)}), f32[4,64,128]{2,1,0:T(8,128)}) %all-reduce.17.cloned.1.call-update) | async-done | bytes 131088 | tf_op jit(solution)/shard_map/psum | solution.py:12
  837.4 0.6 fusion.102
  839.4 41.5 %all-reduce.19.cloned.1.call-done = f32[4,64,128]{2,1,0:T(8,128)} async-done(((f32[4,64,128]{2,1,0:T(8,128)}), f32[4,64,128]{2,1,0:T(8,128)}) %all-reduce.19.cloned.1.call-update) | async-done | bytes 131088 | tf_op jit(solution)/shard_map/psum | solution.py:66
  880.9 1.6 fusion.109
  882.5 1.3 fusion.99
  883.9 1.3 divide_add_fusion.1
  885.2 0.7 convolution_bitcast_fusion.1
  886.3 1.0 gather_fusion.3
  887.7 0.7 select_bitcast_fusion
  888.4 176.1 %all-reduce.21.cloned.1.call-done = f32[4,64,128]{2,1,0:T(8,128)} async-done(((f32[4,64,128]{2,1,0:T(8,128)}), f32[4,64,128]{2,1,0:T(8,128)}) %all-reduce.21.cloned.1.call-update) | async-done | bytes 131088 | tf_op jit(solution)/shard_map/psum | solution.py:12
  1065.2 0.6 fusion.101
  1066.5 41.8 %all-reduce.23.cloned.1.call-done = f32[4,64,128]{2,1,0:T(8,128)} async-done(((f32[4,64,128]{2,1,0:T(8,128)}), f32[4,64,128]{2,1,0:T(8,128)}) %all-reduce.23.cloned.1.call-update) | async-done | bytes 131088 | tf_op jit(solution)/shard_map/psum | solution.py:66
  1108.3 1.6 fusion.110
  1109.9 1.3 fusion.100
  1111.2 1.3 divide_add_fusion
  1112.6 0.7 convolution_bitcast_fusion
  1113.5 30.3 %all_to_all.36 = f32[128,2,512]{2,1,0:T(2,128)S(1)} all-to-all(f32[128,2,512]{2,1,0:T(2,128)S(1)} %copy.39), channel_id=1, replica_groups=mesh['grid'=64,'lev'=4] {'grid'}, dimensions={0} | all-to-all | bytes 1048576 | tf_op jit(solution)/shard_map/all_to_all | solution.py:82
  1143.7 0.8 copy.67
  (53 shorter events, 3.6 us)
Async XLA Ops:
  39.0 62.8 %copy-start.1 = (s32[4,4,64]{2,1,0:T(4,128)S(1)}, s32[4,4,64]{2,1,0:T(4,128)}, u32[]{:S(2)}) copy-start(s32[4,4,64]{2,1,0:T(4,128)} %param.10) | copy-start | bytes 12292
  39.0 63.0 %copy-start.2 = (s32[4]{0:T(128)S(1)}, s32[4]{0:T(128)}, u32[]{:S(2)}) copy-start(s32[4]{0:T(128)} %param.9) | copy-start | bytes 52
  39.0 64.3 %copy-start.4 = (f32[4,1,64]{2,1,0:T(1,128)S(1)}, f32[4,1,64]{2,1,0:T(1,128)}, u32[]{:S(2)}) copy-start(f32[4,1,64]{2,1,0:T(1,128)} %param.12) | copy-start | bytes 3076
  39.0 64.3 %copy-start.5 = (f32[4,1,64]{2,1,0:T(1,128)S(1)}, f32[4,1,64]{2,1,0:T(1,128)}, u32[]{:S(2)}) copy-start(f32[4,1,64]{2,1,0:T(1,128)} %param.11) | copy-start | bytes 3076
  88.5 30.9 %all-to-all-start = ((f32[64,1,2048]{2,1,0:T(1,128)}), f32[64,1,2048]{2,1,0:T(1,128)S(1)}, u32[]{:S(2)}, u32[]{:S(2)}) async-start(f32[64,1,2048]{2,1,0:T(1,128)} %reshape.797), calls=%async_computation | async-start | bytes 1048576 | tf_op jit(solution)/shard_map/all_to_all | solution.py:53
  101.7 281.4 %all-reduce.9.cloned.1.call-start = ((), (), s32[]{:S(2)}) async-start(), calls=%async_computation.2 | async-start | bytes 262144 | tf_op jit(solution)/shard_map/psum | solution.py:12
  175.2 37.3 %copy-start = (f32[2,4]{1,0:T(2,128)S(1)}, f32[2,4]{1,0:T(2,128)}, u32[]{:S(2)}) copy-start(f32[2,4]{1,0:T(2,128)} %param.8) | copy-start | bytes 100
  175.2 38.1 %copy-start.3 = (s32[4,1,1,128]{3,2,1,0:T(1,128)S(1)}, s32[4,1,1,128]{3,2,1,0:T(1,128)}, u32[]{:S(2)}) copy-start(s32[4,1,1,128]{3,2,1,0:T(1,128)} %param.13) | copy-start | bytes 6148
  213.3 213.6 %all-reduce.11.cloned.1.call-start = ((), (), s32[]{:S(2)}) async-start(), calls=%async_computation.3 | async-start | bytes 262144 | tf_op jit(solution)/shard_map/psum | solution.py:66
  383.1 226.7 %all-reduce.13.cloned.1.call-start = ((), (), s32[]{:S(2)}) async-start(), calls=%async_computation.4 | async-start | bytes 262144 | tf_op jit(solution)/shard_map/psum | solution.py:12
  433.8 219.7 %all-reduce.15.cloned.1.call-start = ((), (), s32[]{:S(2)}) async-start(), calls=%async_computation.5 | async-start | bytes 262144 | tf_op jit(solution)/shard_map/psum | solution.py:66
  609.8 227.5 %all-reduce.17.cloned.1.call-start = ((), (), s32[]{:S(2)}) async-start(), calls=%async_computation.6 | async-start | bytes 262144 | tf_op jit(solution)/shard_map/psum | solution.py:12
  661.3 219.6 %all-reduce.19.cloned.1.call-start = ((), (), s32[]{:S(2)}) async-start(), calls=%async_computation.7 | async-start | bytes 262144 | tf_op jit(solution)/shard_map/psum | solution.py:66
  837.4 227.1 %all-reduce.21.cloned.1.call-start = ((), (), s32[]{:S(2)}) async-start(), calls=%async_computation.8 | async-start | bytes 262144 | tf_op jit(solution)/shard_map/psum | solution.py:12
  888.3 220.0 %all-reduce.23.cloned.1.call-start = ((), (), s32[]{:S(2)}) async-start(), calls=%async_computation.9 | async-start | bytes 262144 | tf_op jit(solution)/shard_map/psum | solution.py:66
Sparse Core Ops, SparseCore 0:
  213.4 169.6 all-reduce.8
  385.4 41.3 all-reduce.10
  433.9 175.8 all-reduce.12
  612.1 41.3 all-reduce.14
  661.4 175.8 all-reduce.16
  839.5 41.3 all-reduce.18
  888.5 175.9 all-reduce.20
  1066.9 41.3 all-reduce.22
where the time goes:
time: 1160 us; the launch traced here: 1150 us
  waiting for transfers between devices  878 us (76%)
  local copies, waits for them, and re-layouts  179 us (15%)
  blocking collectives  30.3 us (3%)
  between operations  21.8 us (2%)
  other arithmetic  18.7 us (2%)
  starting transfers between devices  13.7 us (1%)
    psum x4, waiting for transfers between devices, spread(): return lax.psum(kept, axis)  696 us
    psum x4, waiting for transfers between devices, body(): priors = lax.psum(shared, 'lev')  166 us
    unnamed x18, local copies, waits for them, and re-layouts  136 us
    all_to_all x4, local copies, waits for them, and re-layouts, body(): lax.all_to_all(prior_fields, 'grid', split_axis=2, concat_axis=0, tiled=T...  36.7 us
    all_to_all x1, blocking collectives, body(): lax.all_to_all(fields, 'grid', split_axis=0, concat_axis=2, tiled=True)  30.3 us
  transfers between devices with their start and end apart: 9, of which 9 were waited for; matrix products, arithmetic and copies ran while one was open for 0% of the time, Pallas kernels for 0%

commit v1 on v0

--- a/solution.py
+++ b/solution.py
@@ -50,7 +50,15 @@
     region_list = jnp.arange(local_regions, dtype=jnp.int32)
     centres = (block * local_regions + region_list).astype(jnp.float32) + 0.5
     first_cells = obs_offset[0].reshape(-1)
-    fields = lax.all_to_all(prior_fields, "grid", split_axis=2, concat_axis=0, tiled=True)
+    fields = jnp.concatenate(
+        lax.all_to_all(
+            jnp.stack(jnp.split(prior_fields, lax.axis_size("grid"), axis=2), axis=0),
+            axis_name="grid",
+            split_axis=0,
+            concat_axis=0,
+        ),
+        axis=0,
+    )
     picked = fields[:, :, first_cells]
     for batch in range(NB):
         owner = obs_owner[batch]

time: 1160 us -> 1070 us (0.922)
  local copies, waits for them, and re-layouts: 179 us -> 90.7 us
    unnamed x18 -> x76, local copies, waits for them, and re-layouts: 136 us -> 81.8 us
    all_to_all x4 -> x0, local copies, waits for them, and re-layouts: 36.7 us -> none  [body(): lax.all_to_all(prior_fields, 'grid', split_axis=2, concat_axis=0, tiled=T...]
where the time goes in v1:
time: 1070 us; the launch traced here: 1060 us
  waiting for transfers between devices  879 us (82%)
  local copies, waits for them, and re-layouts  90.7 us (8%)
  blocking collectives  30.3 us (3%)
  between operations  21.3 us (2%)
  other arithmetic  17.4 us (2%)
  starting transfers between devices  13.6 us (1%)
    psum x4, waiting for transfers between devices, spread(): return lax.psum(kept, axis)  696 us
    psum x4, waiting for transfers between devices, body(): priors = lax.psum(shared, 'lev')  167 us
    unnamed x76, local copies, waits for them, and re-layouts  81.8 us
    all_to_all x1, blocking collectives, body(): lax.all_to_all(fields, 'grid', split_axis=0, concat_axis=2, tiled=True)  30.3 us
  transfers between devices with their start and end apart: 9, of which 9 were waited for; matrix products, arithmetic and copies ran while one was open for 0% of the time, Pallas kernels for 0%

profile of v1, /device:TPU:1, one launch (start us, length us, event | category | flops | bytes accessed | tf_op | source)
XLA Modules:
  0.0 1061.7 jit_solution(10447274248523467401)
XLA Ops:
  6.5 1.3 constant_dynamic-update-slice_fusion.63
  7.8 1.3 constant_dynamic-update-slice_fusion.62
  10.4 1.3 constant_dynamic-update-slice_fusion.60
  11.7 1.3 constant_dynamic-update-slice_fusion.59
  13.0 1.3 constant_dynamic-update-slice_fusion.58
  14.3 1.3 constant_dynamic-update-slice_fusion.57
  15.6 1.3 constant_dynamic-update-slice_fusion.56
  16.9 1.3 constant_dynamic-update-slice_fusion.55
  19.5 1.3 constant_dynamic-update-slice_fusion.53
  20.8 1.3 constant_dynamic-update-slice_fusion.52
  23.4 1.3 constant_dynamic-update-slice_fusion.50
  24.7 1.3 constant_dynamic-update-slice_fusion.49
  26.0 1.3 constant_dynamic-update-slice_fusion.48
  27.3 1.3 constant_dynamic-update-slice_fusion.47
  28.6 1.3 constant_dynamic-update-slice_fusion.46
  31.1 1.3 constant_dynamic-update-slice_fusion.44
  32.4 1.3 constant_dynamic-update-slice_fusion.43
  33.7 1.3 constant_dynamic-update-slice_fusion.42
  35.0 1.3 constant_dynamic-update-slice_fusion.41
  36.3 1.3 constant_dynamic-update-slice_fusion.40
  37.6 1.3 constant_dynamic-update-slice_fusion.39
  38.9 1.3 constant_dynamic-update-slice_fusion.38
  40.2 1.3 constant_dynamic-update-slice_fusion.37
  46.7 1.3 constant_dynamic-update-slice_fusion.32
  83.0 1.3 constant_dynamic-update-slice_fusion.4
  89.5 13.3 %all-to-all-start = ((f32[64,2,2,512]{3,2,1,0:T(2,128)}), f32[64,2,2,512]{3,2,1,0:T(2,128)S(1)}, u32[]{:S(2)}, u32[]{:S(2)}) async-start(f32[64,2,2,512]{3,2,1,0:T(2,128)} %constant_dynamic-update-slice_fusion), calls=%async_computation | async-start | bytes 1048576 | tf_op jit(solution)/shard_map/all_to_all | solution.py:54
  104.5 16.1 %all-to-all-done = f32[64,2,2,512]{3,2,1,0:T(2,128)S(1)} async-done(((f32[64,2,2,512]{3,2,1,0:T(2,128)}), f32[64,2,2,512]{3,2,1,0:T(2,128)S(1)}, u32[]{:S(2)}, u32[]{:S(2)}) %all-to-all-start) | async-done | bytes 524320 | tf_op jit(solution)/shard_map/all_to_all | solution.py:54
  123.7 169.2 %all-reduce.9.cloned.1.call-done = f32[4,64,128]{2,1,0:T(8,128)} async-done(((f32[4,64,128]{2,1,0:T(8,128)}), f32[4,64,128]{2,1,0:T(8,128)}) %all-reduce.9.cloned.1.call-update) | async-done | bytes 131088 | tf_op jit(solution)/shard_map/psum | solution.py:12
  295.0 41.6 %all-reduce.11.cloned.1.call-done = f32[4,64,128]{2,1,0:T(8,128)} async-done(((f32[4,64,128]{2,1,0:T(8,128)}), f32[4,64,128]{2,1,0:T(8,128)}) %all-reduce.11.cloned.1.call-update) | async-done | bytes 131088 | tf_op jit(solution)/shard_map/psum | solution.py:74
  336.6 1.6 fusion.107
  338.2 1.3 fusion.97
  339.6 1.3 divide_add_fusion.3
  345.0 175.4 %all-reduce.13.cloned.1.call-done = f32[4,64,128]{2,1,0:T(8,128)} async-done(((f32[4,64,128]{2,1,0:T(8,128)}), f32[4,64,128]{2,1,0:T(8,128)}) %all-reduce.13.cloned.1.call-update) | async-done | bytes 131088 | tf_op jit(solution)/shard_map/psum | solution.py:12
  522.5 41.7 %all-reduce.15.cloned.1.call-done = f32[4,64,128]{2,1,0:T(8,128)} async-done(((f32[4,64,128]{2,1,0:T(8,128)}), f32[4,64,128]{2,1,0:T(8,128)}) %all-reduce.15.cloned.1.call-update) | async-done | bytes 131088 | tf_op jit(solution)/shard_map/psum | solution.py:74
  564.2 1.6 fusion.108
  565.8 1.3 fusion.98
  567.1 1.3 divide_add_fusion.2
  572.3 175.4 %all-reduce.17.cloned.1.call-done = f32[4,64,128]{2,1,0:T(8,128)} async-done(((f32[4,64,128]{2,1,0:T(8,128)}), f32[4,64,128]{2,1,0:T(8,128)}) %all-reduce.17.cloned.1.call-update) | async-done | bytes 131088 | tf_op jit(solution)/shard_map/psum | solution.py:12
  749.7 41.6 %all-reduce.19.cloned.1.call-done = f32[4,64,128]{2,1,0:T(8,128)} async-done(((f32[4,64,128]{2,1,0:T(8,128)}), f32[4,64,128]{2,1,0:T(8,128)}) %all-reduce.19.cloned.1.call-update) | async-done | bytes 131088 | tf_op jit(solution)/shard_map/psum | solution.py:74
  791.3 1.6 fusion.109
  792.8 1.3 fusion.99
  794.2 1.3 divide_add_fusion.1
  798.7 176.0 %all-reduce.21.cloned.1.call-done = f32[4,64,128]{2,1,0:T(8,128)} async-done(((f32[4,64,128]{2,1,0:T(8,128)}), f32[4,64,128]{2,1,0:T(8,128)}) %all-reduce.21.cloned.1.call-update) | async-done | bytes 131088 | tf_op jit(solution)/shard_map/psum | solution.py:12
  976.7 41.9 %all-reduce.23.cloned.1.call-done = f32[4,64,128]{2,1,0:T(8,128)} async-done(((f32[4,64,128]{2,1,0:T(8,128)}), f32[4,64,128]{2,1,0:T(8,128)}) %all-reduce.23.cloned.1.call-update) | async-done | bytes 131088 | tf_op jit(solution)/shard_map/psum | solution.py:74
  1018.5 1.6 fusion.110
  1020.1 1.3 fusion.100
  1021.5 1.3 divide_add_fusion
  1023.7 30.3 %all_to_all.23 = f32[128,2,512]{2,1,0:T(2,128)S(1)} all-to-all(f32[128,2,512]{2,1,0:T(2,128)S(1)} %copy.28), channel_id=1, replica_groups=mesh['grid'=64,'lev'=4] {'grid'}, dimensions={0} | all-to-all | bytes 1048576 | tf_op jit(solution)/shard_map/all_to_all | solution.py:90
  (108 shorter events, 68.4 us)
Async XLA Ops:
  89.5 13.4 %copy-start = (s32[4,4,64]{2,1,0:T(4,128)S(1)}, s32[4,4,64]{2,1,0:T(4,128)}, u32[]{:S(2)}) copy-start(s32[4,4,64]{2,1,0:T(4,128)} %param.10) | copy-start | bytes 12292
  89.5 13.6 %copy-start.5 = (f32[2,4]{1,0:T(2,128)S(1)}, f32[2,4]{1,0:T(2,128)}, u32[]{:S(2)}) copy-start(f32[2,4]{1,0:T(2,128)} %param.8) | copy-start | bytes 100
  89.5 13.7 %copy-start.1 = (s32[4]{0:T(128)S(1)}, s32[4]{0:T(128)}, u32[]{:S(2)}) copy-start(s32[4]{0:T(128)} %param.9) | copy-start | bytes 52
  89.5 14.9 %copy-start.3 = (f32[4,1,64]{2,1,0:T(1,128)S(1)}, f32[4,1,64]{2,1,0:T(1,128)}, u32[]{:S(2)}) copy-start(f32[4,1,64]{2,1,0:T(1,128)} %param.12) | copy-start | bytes 3076
  89.5 14.9 %copy-start.4 = (f32[4,1,64]{2,1,0:T(1,128)S(1)}, f32[4,1,64]{2,1,0:T(1,128)}, u32[]{:S(2)}) copy-start(f32[4,1,64]{2,1,0:T(1,128)} %param.11) | copy-start | bytes 3076
  89.5 31.0 %all-to-all-start = ((f32[64,2,2,512]{3,2,1,0:T(2,128)}), f32[64,2,2,512]{3,2,1,0:T(2,128)S(1)}, u32[]{:S(2)}, u32[]{:S(2)}) async-start(f32[64,2,2,512]{3,2,1,0:T(2,128)} %constant_dynamic-update-slice_fusion), calls=%async_computation | async-start | bytes 1048576 | tf_op jit(solution)/shard_map/all_to_all | solution.py:54
  102.8 190.1 %all-reduce.9.cloned.1.call-start = ((), (), s32[]{:S(2)}) async-start(), calls=%async_computation.2 | async-start | bytes 262144 | tf_op jit(solution)/shard_map/psum | solution.py:12
  122.0 1.2 copy-start.2
  123.1 213.6 %all-reduce.11.cloned.1.call-start = ((), (), s32[]{:S(2)}) async-start(), calls=%async_computation.3 | async-start | bytes 262144 | tf_op jit(solution)/shard_map/psum | solution.py:74
  292.9 227.5 %all-reduce.13.cloned.1.call-start = ((), (), s32[]{:S(2)}) async-start(), calls=%async_computation.4 | async-start | bytes 262144 | tf_op jit(solution)/shard_map/psum | solution.py:12
  344.4 219.7 %all-reduce.15.cloned.1.call-start = ((), (), s32[]{:S(2)}) async-start(), calls=%async_computation.5 | async-start | bytes 262144 | tf_op jit(solution)/shard_map/psum | solution.py:74
  520.5 227.2 %all-reduce.17.cloned.1.call-start = ((), (), s32[]{:S(2)}) async-start(), calls=%async_computation.6 | async-start | bytes 262144 | tf_op jit(solution)/shard_map/psum | solution.py:12
  571.6 219.7 %all-reduce.19.cloned.1.call-start = ((), (), s32[]{:S(2)}) async-start(), calls=%async_computation.7 | async-start | bytes 262144 | tf_op jit(solution)/shard_map/psum | solution.py:74
  747.7 227.0 %all-reduce.21.cloned.1.call-start = ((), (), s32[]{:S(2)}) async-start(), calls=%async_computation.8 | async-start | bytes 262144 | tf_op jit(solution)/shard_map/psum | solution.py:12
  798.7 219.9 %all-reduce.23.cloned.1.call-start = ((), (), s32[]{:S(2)}) async-start(), calls=%async_computation.9 | async-start | bytes 262144 | tf_op jit(solution)/shard_map/psum | solution.py:74
Sparse Core Ops, SparseCore 0:
  123.2 169.6 all-reduce.8
  295.2 41.3 all-reduce.10
  344.6 175.8 all-reduce.12
  522.7 41.3 all-reduce.14
  571.7 175.9 all-reduce.16
  749.8 41.3 all-reduce.18
  798.8 175.8 all-reduce.20
  977.1 41.3 all-reduce.22
